TPU v7x, 32 devices: a whole 2x2x4 slice. The times are simulated.
32 devices in a mesh: dp: 4 (over x, core), fsdp: 8 (over z, y).
Axes of the slice: x: 2, y: 2, z: 4, core: 2. Of those that a mesh axis runs over, the one named last changes fastest.
Arguments:
- hidden: bfloat16 [32, 128, 768], P(('dp', 'fsdp')), may hold values from -6 to 6
- sections: int32 [32], P(('dp', 'fsdp')), may hold values from 0 to 3
- lengths: int32 [32], P(('dp', 'fsdp')), may hold values from 32 to 128, as said below
- token_mask: int32 [32, 128], P(('dp', 'fsdp')), may hold values 0 or 1
- cotangent: bfloat16 [32, 128, 768], P(('dp', 'fsdp')), may hold values from -6 to 6
- ln1_gain: bfloat16 [768], P(('dp', 'fsdp')), may hold values from 0.5 to 1.5
- ln1_bias: bfloat16 [768], P(('dp', 'fsdp')), may hold values from -1.5 to 1.5
- qkv_weight: bfloat16 [768, 2304], P(('dp', 'fsdp')), may hold values from -0.21875 to 0.21875
- qv_bias: bfloat16 [1536], P(('dp', 'fsdp')), may hold values from -1.5 to 1.5
- out_weight: bfloat16 [768, 768], P(('dp', 'fsdp')), may hold values from -0.875 to 0.875
- out_bias: bfloat16 [768], P(('dp', 'fsdp')), may hold values from -1.5 to 1.5
- ln2_gain: bfloat16 [768], P(('dp', 'fsdp')), may hold values from 0.5 to 1.5
- ln2_bias: bfloat16 [768], P(('dp', 'fsdp')), may hold values from -1.5 to 1.5
- fc_weight: bfloat16 [768, 3072], P(('dp', 'fsdp')), may hold values from -0.21875 to 0.21875
- fc_bias: bfloat16 [3072], P(('dp', 'fsdp')), may hold values from -1.5 to 1.5
- proj_weight: bfloat16 [3072, 768], P(('dp', 'fsdp')), may hold values from -0.109375 to 0.109375
- proj_bias: bfloat16 [768], P(('dp', 'fsdp')), may hold values from -1.5 to 1.5
Outputs:
- hidden_out: bfloat16 [32, 128, 768], P(('dp', 'fsdp'))
- grad_hidden: float32 [32, 128, 768], P(('dp', 'fsdp'))
- grad_ln1_gain: float32 [768], P(('dp', 'fsdp'))
- grad_ln1_bias: float32 [768], P(('dp', 'fsdp'))
- grad_qkv_weight: float32 [768, 2304], P(('dp', 'fsdp'))
- grad_qv_bias: float32 [1536], P(('dp', 'fsdp'))
- grad_out_weight: float32 [768, 768], P(('dp', 'fsdp'))
- grad_out_bias: float32 [768], P(('dp', 'fsdp'))
- grad_ln2_gain: float32 [768], P(('dp', 'fsdp'))
- grad_ln2_bias: float32 [768], P(('dp', 'fsdp'))
- grad_fc_weight: float32 [768, 3072], P(('dp', 'fsdp'))
- grad_fc_bias: float32 [3072], P(('dp', 'fsdp'))
- grad_proj_weight: float32 [3072, 768], P(('dp', 'fsdp'))
- grad_proj_bias: float32 [768], P(('dp', 'fsdp'))
Inputs may be any that keep to these rules, and one draw needn't show every extreme that they name: `lengths`: some sequence has exactly 128 valid tokens and some has exactly 32.
All inputs are finite; a program needn't handle non-finite values. No bound on the sum of `token_mask` on one device may be relied on, other than what follows from the above.
Results may differ from a plain program's by a relative error of at most 0.013.
Values may be sent and summed in bfloat16 or wider, within the bound.
A program may use at most 192 MiB of HBM per device.

v0:
```python
import jax
import jax.numpy as jnp
from jax import lax
from jax.sharding import PartitionSpec as P

HEAD_DIM = 64
PASSES = 4


epsilon = 1e-05
score_scale = 0.125
gelu_coef = 0.7978845608028654


def layer_norm(values, gain, shift):
    centre = values - jnp.mean(values, axis=-1, keepdims=True)
    spread = jnp.mean(centre * centre, axis=-1, keepdims=True)
    return centre * lax.rsqrt(spread + epsilon) * gain + shift


def gelu_tanh(values):
    return (
        0.5 * values * (1.0 + jnp.tanh(gelu_coef * (values + 0.044715 * values * values * values)))
    )


def fetch_attention(ln1_gain, ln1_bias, qkv_weight, qv_bias, out_weight, out_bias):
    return (
        lax.all_gather(ln1_gain, ("dp", "fsdp"), axis=0, tiled=True),
        lax.all_gather(ln1_bias, ("dp", "fsdp"), axis=0, tiled=True),
        lax.all_gather(qkv_weight, ("dp", "fsdp"), axis=0, tiled=True),
        lax.all_gather(qv_bias, ("dp", "fsdp"), axis=0, tiled=True),
        lax.all_gather(out_weight, ("dp", "fsdp"), axis=0, tiled=True),
        lax.all_gather(out_bias, ("dp", "fsdp"), axis=0, tiled=True),
    )


def fetch_mlp(ln2_gain, ln2_bias, fc_weight, fc_bias, proj_weight, proj_bias):
    return (
        lax.all_gather(ln2_gain, ("dp", "fsdp"), axis=0, tiled=True),
        lax.all_gather(ln2_bias, ("dp", "fsdp"), axis=0, tiled=True),
        lax.all_gather(fc_weight, ("dp", "fsdp"), axis=0, tiled=True),
        lax.all_gather(fc_bias, ("dp", "fsdp"), axis=0, tiled=True),
        lax.all_gather(proj_weight, ("dp", "fsdp"), axis=0, tiled=True),
        lax.all_gather(proj_bias, ("dp", "fsdp"), axis=0, tiled=True),
    )


def allowed_rows(key_valid, block_rows, seq_len):
    query_pos = jnp.arange(block_rows, dtype=jnp.int32)[:, None]
    key_pos = jnp.arange(seq_len, dtype=jnp.int32)[None, :]
    return (key_pos <= query_pos) & (key_valid[:, None, :] | (key_pos == query_pos))


def attend_forward(queries, key_rows, values, key_valid):
    seq_len = queries.shape[1]
    block_rows = min(512, seq_len)
    scores = (
        jnp.einsum("gqhd,gkhd->ghqk", queries, key_rows, preferred_element_type=jnp.float32)
        * score_scale
    )
    allowed = allowed_rows(key_valid, block_rows, seq_len)[:, None]
    scores = jnp.where(allowed, scores, -1e30)
    row_max = jnp.max(scores, axis=-1, keepdims=True)
    expo = jnp.exp(scores - row_max)
    row_total = jnp.sum(expo, axis=-1, keepdims=True)
    probs = (expo / row_total).astype(jnp.bfloat16)
    outputs = jnp.einsum("ghqk,gkhd->gqhd", probs, values, preferred_element_type=jnp.float32)
    totals = (row_max + jnp.log(row_total))[..., 0]
    return (outputs, totals)


def attend_backward(queries, key_rows, values, log_totals, grad_mixed, key_valid):
    seq_len = queries.shape[1]
    block_rows = min(512, seq_len)
    scores = (
        jnp.einsum("gqhd,gkhd->ghqk", queries, key_rows, preferred_element_type=jnp.float32)
        * score_scale
    )
    allowed = allowed_rows(key_valid, block_rows, seq_len)[:, None]
    block_totals = log_totals[:, :, 0:block_rows, None]
    probs = jnp.where(allowed, jnp.exp(scores - block_totals), 0.0)
    probs_low = probs.astype(jnp.bfloat16)
    grad_values = jnp.einsum(
        "ghqk,gqhd->gkhd", probs_low, grad_mixed, preferred_element_type=jnp.float32
    )
    grad_probs = jnp.einsum(
        "gqhd,gkhd->ghqk", grad_mixed, values, preferred_element_type=jnp.float32
    )
    inner = jnp.sum(grad_probs * probs, axis=-1, keepdims=True)
    grad_scores = (probs * (grad_probs - inner)).astype(jnp.bfloat16)
    grad_queries = (
        jnp.einsum("ghqk,gkhd->gqhd", grad_scores, key_rows, preferred_element_type=jnp.float32)
        * score_scale
    )
    grad_keys = (
        jnp.einsum("ghqk,gqhd->gkhd", grad_scores, queries, preferred_element_type=jnp.float32)
        * score_scale
    )
    return (grad_queries, grad_keys, grad_values)


def forward_pass(state, weights, key_valid, live, seq_count, seq_len):
    (gain_one, shift_one, qkv_w, qv_b, out_w, out_b), (
        gain_two,
        shift_two,
        fc_w,
        fc_b,
        proj_w,
        proj_b,
    ) = weights
    row_count, model_width = state.shape
    head_count = model_width // HEAD_DIM
    normed = layer_norm(state, gain_one.astype(jnp.float32), shift_one.astype(jnp.float32)).astype(
        jnp.bfloat16
    )
    qv_float = qv_b.astype(jnp.float32)
    bias_full = jnp.concatenate(
        [qv_float[:model_width], jnp.zeros((model_width,), jnp.float32), qv_float[model_width:]]
    )
    joined = (jnp.dot(normed, qkv_w, preferred_element_type=jnp.float32) + bias_full).astype(
        jnp.bfloat16
    )
    split = joined.reshape(seq_count, seq_len, 3, head_count, HEAD_DIM)
    queries = split[:, :, 0]
    key_rows = split[:, :, 1]
    values = split[:, :, 2]
    mixed_float, log_totals = attend_forward(queries, key_rows, values, key_valid)
    mixed = mixed_float.reshape(row_count, model_width).astype(jnp.bfloat16)
    middle = (
        state
        + jnp.dot(mixed, out_w, preferred_element_type=jnp.float32)
        + out_b.astype(jnp.float32)
    )
    normed_two = layer_norm(
        middle, gain_two.astype(jnp.float32), shift_two.astype(jnp.float32)
    ).astype(jnp.bfloat16)
    upper = jnp.dot(normed_two, fc_w, preferred_element_type=jnp.float32) + fc_b.astype(jnp.float32)
    activated = gelu_tanh(upper).astype(jnp.bfloat16)
    result = (
        middle
        + jnp.dot(activated, proj_w, preferred_element_type=jnp.float32)
        + proj_b.astype(jnp.float32)
    )
    record = (
        state,
        normed,
        queries,
        key_rows,
        values,
        log_totals,
        mixed,
        middle,
        normed_two,
        upper,
        activated,
    )
    return (jnp.where(live, result, state), record)


def backward_mlp(grad_next, record, weights, live):
    (
        state,
        normed,
        queries,
        key_rows,
        values,
        log_totals,
        mixed,
        middle,
        normed_two,
        upper,
        activated,
    ) = record
    (gain_one, shift_one, qkv_w, qv_b, out_w, out_b), (
        gain_two,
        shift_two,
        fc_w,
        fc_b,
        proj_w,
        proj_b,
    ) = weights
    grad_out = jnp.where(live, grad_next, 0.0)
    grad_branch = grad_out.astype(jnp.bfloat16)
    term_proj_b = jnp.sum(grad_branch.astype(jnp.float32), axis=0)
    term_proj_w = jnp.einsum(
        "ti,to->io", activated, grad_branch, preferred_element_type=jnp.float32
    )
    grad_act = jnp.einsum("to,io->ti", grad_branch, proj_w, preferred_element_type=jnp.float32)
    gelu_pull = jax.vjp(gelu_tanh, upper)[1]
    grad_upper = gelu_pull(grad_act)[0].astype(jnp.bfloat16)
    term_fc_b = jnp.sum(grad_upper.astype(jnp.float32), axis=0)
    term_fc_w = jnp.einsum("td,tf->df", normed_two, grad_upper, preferred_element_type=jnp.float32)
    grad_normed_two = jnp.einsum("tf,df->td", grad_upper, fc_w, preferred_element_type=jnp.float32)
    norm_pull_two = jax.vjp(
        layer_norm, middle, gain_two.astype(jnp.float32), shift_two.astype(jnp.float32)
    )[1]
    grad_mid_norm, term_gain_two, term_shift_two = norm_pull_two(grad_normed_two)
    grad_middle = grad_out + grad_mid_norm
    mlp_terms = (term_gain_two, term_shift_two, term_fc_w, term_fc_b, term_proj_w, term_proj_b)
    return (grad_middle, mlp_terms)


def backward_attention(grad_next, grad_middle, record, weights, key_valid, live):
    (
        state,
        normed,
        queries,
        key_rows,
        values,
        log_totals,
        mixed,
        middle,
        normed_two,
        upper,
        activated,
    ) = record
    (gain_one, shift_one, qkv_w, qv_b, out_w, out_b), mlp_weights = weights
    row_count, model_width = state.shape
    grad_attn = grad_middle.astype(jnp.bfloat16)
    term_out_b = jnp.sum(grad_attn.astype(jnp.float32), axis=0)
    term_out_w = jnp.einsum("td,te->de", mixed, grad_attn, preferred_element_type=jnp.float32)
    grad_mixed = jnp.einsum(
        "te,de->td", grad_attn, out_w, preferred_element_type=jnp.float32
    ).astype(jnp.bfloat16)
    grad_mixed = grad_mixed.reshape(queries.shape)
    grad_queries, grad_keys, grad_values = attend_backward(
        queries, key_rows, values, log_totals, grad_mixed, key_valid
    )
    grad_joined = (
        jnp.stack([grad_queries, grad_keys, grad_values], axis=2)
        .reshape(row_count, 3 * model_width)
        .astype(jnp.bfloat16)
    )
    column_sums = jnp.sum(grad_joined.astype(jnp.float32), axis=0)
    term_qv_b = jnp.concatenate([column_sums[:model_width], column_sums[2 * model_width :]])
    term_qkv_w = jnp.einsum("td,tk->dk", normed, grad_joined, preferred_element_type=jnp.float32)
    grad_normed = jnp.einsum("tk,dk->td", grad_joined, qkv_w, preferred_element_type=jnp.float32)
    norm_pull_one = jax.vjp(
        layer_norm, state, gain_one.astype(jnp.float32), shift_one.astype(jnp.float32)
    )[1]
    grad_state_norm, term_gain_one, term_shift_one = norm_pull_one(grad_normed)
    grad_prev = grad_middle + grad_state_norm + jnp.where(live, 0.0, grad_next)
    attention_terms = (term_gain_one, term_shift_one, term_qkv_w, term_qv_b, term_out_w, term_out_b)
    return (grad_prev, attention_terms)


def body(
    hidden,
    sections,
    lengths,
    token_mask,
    cotangent,
    ln1_gain,
    ln1_bias,
    qkv_weight,
    qv_bias,
    out_weight,
    out_bias,
    ln2_gain,
    ln2_bias,
    fc_weight,
    fc_bias,
    proj_weight,
    proj_bias,
):
    seq_count, seq_len, model_width = hidden.shape
    row_count = seq_count * seq_len
    key_pos = jnp.arange(seq_len, dtype=jnp.int32)
    key_valid = (key_pos[None, :] < lengths[:, None]) & (token_mask == 1)

    def gather_both():
        return (
            fetch_attention(ln1_gain, ln1_bias, qkv_weight, qv_bias, out_weight, out_bias),
            fetch_mlp(ln2_gain, ln2_bias, fc_weight, fc_bias, proj_weight, proj_bias),
        )

    state = hidden.reshape(row_count, model_width).astype(jnp.float32)
    records = []
    for section_index in range(PASSES):
        current = gather_both()
        live = jnp.repeat(sections >= section_index, seq_len)[:, None]
        state, record = forward_pass(state, current, key_valid, live, seq_count, seq_len)
        records.append(record)
    hidden_out = state.astype(jnp.bfloat16).reshape(seq_count, seq_len, model_width)
    grad_state = cotangent.reshape(row_count, model_width).astype(jnp.float32)
    attention_sum = None
    mlp_sum = None
    for section_index in reversed(range(PASSES)):
        current = gather_both()
        live = jnp.repeat(sections >= section_index, seq_len)[:, None]
        grad_middle, mlp_terms = backward_mlp(grad_state, records[section_index], current, live)
        if mlp_sum is None:
            mlp_sum = mlp_terms
        else:
            mlp_sum = jax.tree.map(jnp.add, mlp_sum, mlp_terms)
        grad_state, attention_terms = backward_attention(
            grad_state, grad_middle, records[section_index], current, key_valid, live
        )
        if attention_sum is None:
            attention_sum = attention_terms
        else:
            attention_sum = jax.tree.map(jnp.add, attention_sum, attention_terms)
    sum_gain_one, sum_shift_one, sum_qkv_w, sum_qv_b, sum_out_w, sum_out_b = attention_sum
    attention_grads = (
        lax.psum_scatter(sum_gain_one, ("dp", "fsdp"), scatter_dimension=0, tiled=True),
        lax.psum_scatter(sum_shift_one, ("dp", "fsdp"), scatter_dimension=0, tiled=True),
        lax.psum_scatter(sum_qkv_w, ("dp", "fsdp"), scatter_dimension=0, tiled=True),
        lax.psum_scatter(sum_qv_b, ("dp", "fsdp"), scatter_dimension=0, tiled=True),
        lax.psum_scatter(sum_out_w, ("dp", "fsdp"), scatter_dimension=0, tiled=True),
        lax.psum_scatter(sum_out_b, ("dp", "fsdp"), scatter_dimension=0, tiled=True),
    )
    sum_gain_two, sum_shift_two, sum_fc_w, sum_fc_b, sum_proj_w, sum_proj_b = mlp_sum
    finished = (
        lax.psum_scatter(sum_gain_two, ("dp", "fsdp"), scatter_dimension=0, tiled=True),
        lax.psum_scatter(sum_shift_two, ("dp", "fsdp"), scatter_dimension=0, tiled=True),
        lax.psum_scatter(sum_fc_w, ("dp", "fsdp"), scatter_dimension=0, tiled=True),
        lax.psum_scatter(sum_fc_b, ("dp", "fsdp"), scatter_dimension=0, tiled=True),
        lax.psum_scatter(sum_proj_w, ("dp", "fsdp"), scatter_dimension=0, tiled=True),
        lax.psum_scatter(sum_proj_b, ("dp", "fsdp"), scatter_dimension=0, tiled=True),
    )
    grad_hidden = grad_state.reshape(seq_count, seq_len, model_width)
    return (
        hidden_out,
        grad_hidden,
        attention_grads[0],
        attention_grads[1],
        attention_grads[2],
        attention_grads[3],
        attention_grads[4],
        attention_grads[5],
        finished[0],
        finished[1],
        finished[2],
        finished[3],
        finished[4],
        finished[5],
    )


def solution(mesh):
    return jax.shard_map(
        body,
        mesh=mesh,
        in_specs=(
            P(("dp", "fsdp"), None, None),
            P(("dp", "fsdp")),
            P(("dp", "fsdp")),
            P(("dp", "fsdp"), None),
            P(("dp", "fsdp"), None, None),
            P(("dp", "fsdp")),
            P(("dp", "fsdp")),
            P(("dp", "fsdp"), None),
            P(("dp", "fsdp")),
            P(("dp", "fsdp"), None),
            P(("dp", "fsdp")),
            P(("dp", "fsdp")),
            P(("dp", "fsdp")),
            P(("dp", "fsdp"), None),
            P(("dp", "fsdp")),
            P(("dp", "fsdp"), None),
            P(("dp", "fsdp")),
        ),
        out_specs=(
            P(("dp", "fsdp"), None, None),
            P(("dp", "fsdp"), None, None),
            P(("dp", "fsdp")),
            P(("dp", "fsdp")),
            P(("dp", "fsdp"), None),
            P(("dp", "fsdp")),
            P(("dp", "fsdp"), None),
            P(("dp", "fsdp")),
            P(("dp", "fsdp")),
            P(("dp", "fsdp")),
            P(("dp", "fsdp"), None),
            P(("dp", "fsdp")),
            P(("dp", "fsdp"), None),
            P(("dp", "fsdp")),
        ),
        check_vma=False,
    )
```

profile of v0, /device:TPU:0, one launch (start us, length us, event | category | flops | bytes accessed | tf_op | source)
XLA Modules:
  0.0 899.9 jit_solution(807125739731733085)
XLA Ops:
  18.1 43.0 %all-reduce.17 = (bf16[1536]{0:T(1024)(128)(2,1)S(1)}, bf16[768]{0:T(1024)(128)(2,1)S(1)}, bf16[768]{0:T(1024)(128)(2,1)S(1)}, bf16[768]{0:T(1024)(128)(2,1)S(1)...) all-reduce(bf16[1536]{0:T(1024)(128)(2,1)S(1)} %dynamic-update-slic, ...), channel_id=1, replica_groups=mesh['dp'=4,'fsdp'=8] {'dp','fsdp'}, use_global_device_ids=true, to_apply=%add.2 | all-reduce | flops 9216 | bytes 36864
  64.7 9.0 %all-gather.5.cloned.1.call-done = bf16[768,2304]{1,0:T(8,128)(2,1)} async-done(((bf16[24,2304]{1,0:T(8,128)(2,1)}), bf16[768,2304]{1,0:T(8,128)(2,1)}) %all-gather.5.cloned.1.call-update) | async-done | bytes 3538960 | tf_op jit(solution)/shard_map/all_gather | solution.py:31
  73.8 2.8 fusion
  78.5 51.2 %all-gather.7.cloned.1.call-done = bf16[768,768]{1,0:T(8,128)(2,1)} async-done(((bf16[24,768]{1,0:T(8,128)(2,1)}), bf16[768,768]{1,0:T(8,128)(2,1)}) %all-gather.7.cloned.1.call-update) | async-done | bytes 1179664 | tf_op jit(solution)/shard_map/all_gather | solution.py:33
  129.7 1.7 fusion.176
  132.3 62.8 %all-gather.9.cloned.1.call-done = bf16[768,3072]{1,0:T(8,128)(2,1)} async-done(((bf16[24,3072]{1,0:T(8,128)(2,1)}), bf16[768,3072]{1,0:T(8,128)(2,1)}) %all-gather.9.cloned.1.call-update) | async-done | bytes 4718608 | tf_op jit(solution)/shard_map/all_gather | solution.py:42
  195.1 3.2 convolution_add_fusion.7
  198.3 61.4 %all-gather.11.cloned.1.call-done = bf16[3072,768]{1,0:T(8,128)(2,1)} async-done(((bf16[96,768]{1,0:T(8,128)(2,1)}), bf16[3072,768]{1,0:T(8,128)(2,1)}) %all-gather.11.cloned.1.call-update) | async-done | bytes 4718608 | tf_op jit(solution)/shard_map/all_gather | solution.py:44
  259.7 3.6 fusion.177
  266.2 1.6 copy-done.2
  269.6 4.1 fusion.179
  274.9 1.5 fusion.2
  276.5 2.1 copy.95
  280.8 1.4 convolution_convert_fusion.5
  283.0 3.2 convolution_add_fusion.5
  286.3 4.3 fusion.181
  291.9 1.5 fusion.3
  293.4 2.1 copy.97
  297.7 1.4 convolution_convert_fusion.4
  299.9 3.3 convolution_add_fusion.4
  303.3 5.8 convert_reduce_fusion.3
  309.2 2.3 multiply_reduce_fusion.7
  315.2 1.7 copy.99
  316.9 1.6 convolution_bitcast_fusion.3
  318.6 1.4 multiply_reduce_fusion.3
  321.9 2.0 multiply_reduce_fusion.10
  325.3 5.8 convert_reduce_fusion.2
  331.2 2.5 multiply_reduce_fusion.6
  336.7 1.7 copy.103
  338.4 1.6 convolution_bitcast_fusion.2
  340.0 1.4 multiply_reduce_fusion.2
  343.4 2.0 multiply_reduce_fusion.9
  347.0 3.0 convert_reduce_fusion.1
  350.1 2.3 multiply_reduce_fusion.5
  355.3 1.7 copy.107
  357.0 1.6 convolution_bitcast_fusion.1
  358.7 1.4 multiply_reduce_fusion.1
  361.2 1.9 fusion.185
  363.1 1.9 fusion.184
  365.0 1.9 fusion.183
  368.0 2.0 multiply_reduce_fusion.8
  371.6 3.0 convert_reduce_fusion
  374.6 2.3 multiply_reduce_fusion.4
  379.9 1.7 copy.111
  381.6 5.2 add_add_fusion.3
  386.9 1.8 multiply_reduce_fusion
  390.0 1.7 convert_reduce_fusion.4
  395.6 5.2 add_add_fusion.2
  401.2 6.7 fusion.153
  407.9 5.3 fusion.154
  413.2 1.6 fusion.118
  414.7 11.7 %add_add_fusion = f32[3072,768]{1,0:T(8,128)} fusion(f32[3072,768]{1,0:T(8,128)} %fusion.153, f32[3072,768]{1,0:T(8,128)S(1)} %fusion.118, f32[3072,768]{1,0:T(8,128)} %fusion.154, bf16[128,768]{1,0:T(8,128)(2,1)} %copy-done.123, f32[128,3072]{1,0:T(8,128)S(1)} %copy-done.53), kind=kOutput, calls=%fused_computation | convolution fusion | flops 614596608 | bytes 39518208 | tf_op jit(solution)/shard_map/ti,to->io/dot_general | solution.py:186
  427.1 2.8 fusion.148
  430.1 5.2 fusion.150
  435.3 5.1 fusion.152
  440.4 12.2 %add_add_fusion.1 = f32[768,3072]{1,0:T(8,128)} fusion(f32[768,3072]{1,0:T(8,128)S(1)} %fusion.148, f32[768,3072]{1,0:T(8,128)} %fusion.152, f32[768,3072]{1,0:T(8,128)} %fusion.150, bf16[128,3072]{1,0:T(8,128)(2,1)S(1)} %copy-done.79, f32[128,768]{1,0:T(8,128)S(1)} %copy-done.31, f32[768]{0:T(1024)S(1)} %copy-done.115, f32[768]{0:T(1024)S(1)} %copy-done.94, ...), kind=kOutput, calls=%fused_computation.1 | convolution fusion | flops 611549184 | bytes 38935552 | tf_op jit(solution)/shard_map/td,tf->df/dot_general | solution.py:193
  453.9 1.4 slice.111
  467.0 2.5 fusion.155
  470.6 40.0 %all-reduce.16 = (f32[768]{0:T(1024)S(1)}, f32[768]{0:T(1024)S(1)}, f32[1536]{0:T(1024)S(1)}, f32[768]{0:T(1024)S(1)}, f32[768]{0:T(1024)S(1)}, /*index=5*/f32[7...) all-reduce(f32[768]{0:T(1024)S(1)} %get-tuple-element.154, ...), channel_id=2, replica_groups=mesh['dp'=4,'fsdp'=8] {'dp','fsdp'}, use_global_device_ids=true, to_apply=%region_48.49.clone | all-reduce | flops 9216 | bytes 73728
  515.3 2.4 add_bitcast_fusion
  517.7 4.2 fusion.49
  521.9 87.8 %reduce-scatter.5.cloned.1.call-done = f32[24,2304]{1,0:T(8,128)} async-done(((f32[768,2304]{1,0:T(8,128)}), f32[24,2304]{1,0:T(8,128)}) %reduce-scatter.5.cloned.1.call-update) | async-done | bytes 221200 | tf_op jit(solution)/shard_map/reduce_scatter | solution.py:308
  609.7 141.6 %reduce-scatter.11.cloned.1.call-done = f32[96,768]{1,0:T(8,128)} async-done(((f32[3072,768]{1,0:T(8,128)}), f32[96,768]{1,0:T(8,128)}) %reduce-scatter.11.cloned.1.call-update) | async-done | bytes 294928 | tf_op jit(solution)/shard_map/reduce_scatter | solution.py:319
  751.3 141.6 %reduce-scatter.9.cloned.1.call-done = f32[24,3072]{1,0:T(8,128)} async-done(((f32[768,3072]{1,0:T(8,128)}), f32[24,3072]{1,0:T(8,128)}) %reduce-scatter.9.cloned.1.call-update) | async-done | bytes 294928 | tf_op jit(solution)/shard_map/reduce_scatter | solution.py:317
  (678 shorter events, 75.1 us)
Async XLA Ops:
  7.2 66.6 %all-gather.5.cloned.1.call-start = ((), (), s32[]{:S(2)}) async-start(), calls=%async_computation.4 | async-start | bytes 3649536 | tf_op jit(solution)/shard_map/all_gather | solution.py:31
  7.9 121.8 %all-gather.7.cloned.1.call-start = ((), (), s32[]{:S(2)}) async-start(), calls=%async_computation.5 | async-start | bytes 1216512 | tf_op jit(solution)/shard_map/all_gather | solution.py:33
  8.7 186.4 %all-gather.9.cloned.1.call-start = ((), (), s32[]{:S(2)}) async-start(), calls=%async_computation.6 | async-start | bytes 4866048 | tf_op jit(solution)/shard_map/all_gather | solution.py:42
  9.4 250.3 %all-gather.11.cloned.1.call-start = ((), (), s32[]{:S(2)}) async-start(), calls=%async_computation.7 | async-start | bytes 4866048 | tf_op jit(solution)/shard_map/all_gather | solution.py:44
  10.0 511.9 %reduce-scatter.7.cloned.1.call-start = ((), (), s32[]{:S(2)}) async-start(), calls=%async_computation.9 | async-start | bytes 2433024 | tf_op jit(solution)/shard_map/reduce_scatter | solution.py:310
  61.0 202.5 %copy-start.80 = (f32[768]{0:T(1024)}, f32[768]{0:T(1024)S(1)}, u32[]{:S(2)}) copy-start(f32[768]{0:T(1024)S(1)} %convert_element_type.407) | copy-start | bytes 9220
  61.1 207.4 %copy-start.88 = (f32[768]{0:T(1024)}, f32[768]{0:T(1024)S(1)}, u32[]{:S(2)}) copy-start(f32[768]{0:T(1024)S(1)} %convert_element_type.418) | copy-start | bytes 9220
  61.1 202.5 %copy-start.116 = (f32[768]{0:T(1024)}, f32[768]{0:T(1024)S(1)}, u32[]{:S(2)}) copy-start(f32[768]{0:T(1024)S(1)} %convert_element_type.408) | copy-start | bytes 9220
  61.1 207.4 %copy-start.112 = (f32[768]{0:T(1024)}, f32[768]{0:T(1024)S(1)}, u32[]{:S(2)}) copy-start(f32[768]{0:T(1024)S(1)} %convert_element_type.419) | copy-start | bytes 9220
  61.1 205.0 %copy-start.141 = (f32[768]{0:T(1024)}, f32[768]{0:T(1024)S(1)}, u32[]{:S(2)}) copy-start(f32[768]{0:T(1024)S(1)} %convert_element_type.417) | copy-start | bytes 9220
  61.7 206.8 %copy-start.131 = (f32[3072]{0:T(1024)}, f32[3072]{0:T(1024)S(1)}, u32[]{:S(2)}) copy-start(f32[3072]{0:T(1024)S(1)} %convert_element_type.421) | copy-start | bytes 36868
  61.8 201.8 %copy-start.134 = (f32[2304]{0:T(1024)}, f32[2304]{0:T(1024)S(1)}, u32[]{:S(2)}) copy-start(f32[2304]{0:T(1024)S(1)} %pad_maximum_fusion) | copy-start | bytes 27652
  62.8 13.7 %copy-start.161 = (f32[128]{0:T(128)}, f32[128]{0:T(128)S(1)}, u32[]{:S(2)}) copy-start(f32[128]{0:T(128)S(1)} %broadcast_multiply_fusion.7) | copy-start | bytes 1540
  64.0 12.6 %copy-start.226 = (f32[128]{0:T(128)}, f32[128]{0:T(128)S(1)}, u32[]{:S(2)}) copy-start(f32[128]{0:T(128)S(1)} %fusion.77) | copy-start | bytes 1540
  64.0 12.6 %copy-start.212 = (f32[128]{0:T(128)}, f32[128]{0:T(128)S(1)}, u32[]{:S(2)}) copy-start(f32[128]{0:T(128)S(1)} %fusion.128) | copy-start | bytes 1540
  78.2 51.5 %copy-start.32 = (bf16[1,128,768]{2,1,0:T(8,128)(2,1)S(1)}, bf16[1,128,768]{2,1,0:T(8,128)(2,1)}, u32[]{:S(2)}) copy-start(bf16[1,128,768]{2,1,0:T(8,128)(2,1)} %param.17) | copy-start | bytes 589828
  78.5 119.8 %copy-start.124 = (bf16[12,64,128]{2,1,0:T(8,128)(2,1)}, bf16[12,64,128]{2,1,0:T(8,128)(2,1)S(1)}, u32[]{:S(2)}) copy-start(bf16[12,64,128]{2,1,0:T(8,128)(2,1)S(1)} %convolution_convert_fusion.7) | copy-start | bytes 589828
  131.4 128.3 %copy-start.29 = (f32[128,768]{1,0:T(8,128)}, f32[128,768]{1,0:T(8,128)S(1)}, u32[]{:S(2)}) copy-start(f32[128,768]{1,0:T(8,128)S(1)} %get-tuple-element.114) | copy-start | bytes 1179652
  131.4 66.8 %copy-start.186 = (f32[128]{0:T(128)}, f32[128]{0:T(128)S(1)}, u32[]{:S(2)}) copy-start(f32[128]{0:T(128)S(1)} %broadcast_multiply_fusion.6) | copy-start | bytes 1540
  131.6 66.6 %copy-start.228 = (f32[128]{0:T(128)}, f32[128]{0:T(128)S(1)}, u32[]{:S(2)}) copy-start(f32[128]{0:T(128)S(1)} %multiply_reduce_fusion.24) | copy-start | bytes 1540
  131.7 66.6 %copy-start.209 = (f32[128]{0:T(128)}, f32[128]{0:T(128)S(1)}, u32[]{:S(2)}) copy-start(f32[128]{0:T(128)S(1)} %fusion.129) | copy-start | bytes 1540
  132.3 127.4 %copy-start.215 = (f32[768]{0:T(1024)S(1)}, f32[768]{0:T(1024)}, u32[]{:S(2)}) copy-start(f32[768]{0:T(1024)} %convert_element_type.423) | copy-start | bytes 9220
  198.3 65.0 %copy-start.51 = (f32[128,3072]{1,0:T(8,128)}, f32[128,3072]{1,0:T(8,128)S(1)}, u32[]{:S(2)}) copy-start(f32[128,3072]{1,0:T(8,128)S(1)} %convolution_add_fusion.7) | copy-start | bytes 4718596
  263.4 5.1 slice-start
  269.5 5.4 copy-start.1
  269.5 5.4 copy-start.81
  269.5 5.4 copy-start.117
  269.5 5.4 copy-start.135
  286.3 5.6 copy-start.82
  286.3 5.6 copy-start.118
  286.3 5.6 copy-start.136
  299.6 11.9 %copy-start.21 = (f32[128,768]{1,0:T(8,128)}, f32[128,768]{1,0:T(8,128)S(1)}, u32[]{:S(2)}) copy-start(f32[128,768]{1,0:T(8,128)S(1)} %get-tuple-element.132) | copy-start | bytes 1179652
  299.7 11.9 %copy-start.153 = (f32[128]{0:T(128)}, f32[128]{0:T(128)S(1)}, u32[]{:S(2)}) copy-start(f32[128]{0:T(128)S(1)} %broadcast_multiply_fusion) | copy-start | bytes 1540
  299.9 11.6 %copy-start.197 = (f32[128]{0:T(128)}, f32[128]{0:T(128)S(1)}, u32[]{:S(2)}) copy-start(f32[128]{0:T(128)S(1)} %fusion.135) | copy-start | bytes 1540
  299.9 9.3 %slice-start.2 = ((s8[4718592]{0:T(1024)(128)(4,1)}), s8[4194304]{0:T(1024)(128)(4,1)S(1)}, s32[]{:S(2)}) async-start(s8[4718592]{0:T(1024)(128)(4,1)} %bitcast.341), calls=%async_computation.14 | async-start | bytes 8388608
  303.3 5.9 copy-start.43
  303.3 5.9 slice-start.3
  324.2 6.9 slice-start.4
  325.0 6.1 copy-start.120
  325.0 9.0 %copy-start.62 = (f32[128,768]{1,0:T(8,128)}, f32[128,768]{1,0:T(8,128)S(1)}, u32[]{:S(2)}) copy-start(f32[128,768]{1,0:T(8,128)S(1)} %get-tuple-element.57) | copy-start | bytes 1179652
  325.3 5.8 slice-start.5
  325.3 5.8 copy-start.27
  325.3 5.8 copy-start.91
  325.3 5.8 copy-start.148
  325.3 5.8 copy-start.192
  346.5 6.2 copy-start.60
  371.5 5.7 copy-start.70
  386.8 222.9 %reduce-scatter.5.cloned.1.call-start = ((), (), s32[]{:S(2)}) async-start(), calls=%async_computation.8 | async-start | bytes 7299072 | tf_op jit(solution)/shard_map/reduce_scatter | solution.py:308
  400.9 350.4 %reduce-scatter.11.cloned.1.call-start = ((), (), s32[]{:S(2)}) async-start(), calls=%async_computation.11 | async-start | bytes 9732096 | tf_op jit(solution)/shard_map/reduce_scatter | solution.py:319
  401.1 6.7 copy-start.50
  401.1 6.7 copy-start.121
  407.9 5.3 copy-start.44
  407.9 5.3 copy-start.103
  426.5 466.4 %reduce-scatter.9.cloned.1.call-start = ((), (), s32[]{:S(2)}) async-start(), calls=%async_computation.10 | async-start | bytes 9732096 | tf_op jit(solution)/shard_map/reduce_scatter | solution.py:317
  430.0 5.3 copy-start.22
  430.0 5.2 copy-start.74
  430.0 5.2 copy-start.154
  430.0 5.2 copy-start.198
  452.6 14.1 %copy-start.87 = (f32[768]{0:T(1024)S(1)}, f32[768]{0:T(1024)}, u32[]{:S(2)}) copy-start(f32[768]{0:T(1024)} %copy-done.80) | copy-start | bytes 9220
  452.6 14.1 %copy-start.163 = (f32[128]{0:T(128)S(1)}, f32[128]{0:T(128)}, u32[]{:S(2)}) copy-start(f32[128]{0:T(128)} %copy-done.161) | copy-start | bytes 1540
  469.5 48.1 %copy-start.12 = (f32[128,768]{1,0:T(8,128)S(1)}, f32[128,768]{1,0:T(8,128)}, u32[]{:S(2)}) copy-start(f32[128,768]{1,0:T(8,128)} %copy-done.8) | copy-start | bytes 1179652
  469.5 48.1 %copy-start.23 = (f32[128,768]{1,0:T(8,128)S(1)}, f32[128,768]{1,0:T(8,128)}, u32[]{:S(2)}) copy-start(f32[128,768]{1,0:T(8,128)} %copy-done.21) | copy-start | bytes 1179652
  469.5 48.1 %copy-start.45 = (f32[128,3072]{1,0:T(8,128)S(1)}, f32[128,3072]{1,0:T(8,128)}, u32[]{:S(2)}) copy-start(f32[128,3072]{1,0:T(8,128)} %copy-done.43) | copy-start | bytes 4718596
  469.5 48.1 %copy-start.218 = (f32[768]{0:T(1024)S(1)}, f32[768]{0:T(1024)}, u32[]{:S(2)}) copy-start(f32[768]{0:T(1024)} %convert_element_type.423) | copy-start | bytes 9220
  (196 other events, 437.9 us)
Sparse Core Ops, SparseCore 0:
  10.9 62.8 all-gather.4
  76.7 52.9 all-gather.6
  132.6 62.3 all-gather.8
  197.8 61.8 all-gather.10
  386.9 97.9 reduce-scatter.6
  491.1 118.5 reduce-scatter.4
  616.1 135.0 reduce-scatter.10
  757.7 135.1 reduce-scatter.8
where the time goes:
time: 904 us; the launch traced here: 900 us
  waiting for transfers between devices  558 us (62%)
  matrix products  168 us (19%)
  blocking collectives  83 us (9%)
  local copies, waits for them, and re-layouts  47.5 us (5%)
  other arithmetic  24.3 us (3%)
  between operations  19 us (2%)
    reduce_scatter x1, waiting for transfers between devices, body(): lax.psum_scatter(sum_fc_w, ('dp', 'fsdp'), scatter_dimension=0, tiled=True)  142 us
    reduce_scatter x1, waiting for transfers between devices, body(): lax.psum_scatter(sum_proj_w, ('dp', 'fsdp'), scatter_dimension=0, tiled=T...  142 us
    reduce_scatter x1, waiting for transfers between devices, body(): lax.psum_scatter(sum_qkv_w, ('dp', 'fsdp'), scatter_dimension=0, tiled=True)  87.8 us
    unnamed x2, blocking collectives  83 us
    all_gather x1, waiting for transfers between devices, fetch_mlp(): lax.all_gather(fc_weight, ('dp', 'fsdp'), axis=0, tiled=True)  62.8 us
    all_gather x1, waiting for transfers between devices, fetch_mlp(): lax.all_gather(proj_weight, ('dp', 'fsdp'), axis=0, tiled=True)  61.4 us
    all_gather x1, waiting for transfers between devices, fetch_attention(): lax.all_gather(out_weight, ('dp', 'fsdp'), axis=0, tiled=True)  51.2 us
    dot_general x4, matrix products, backward_mlp(): jnp.einsum('td,tf->df', normed_two, grad_upper, preferred_element_type=jn...  25.3 us
  transfers between devices with their start and end apart: 8, of which 7 were waited for; matrix products, arithmetic and copies ran while one was open for 12% of the time, Pallas kernels for 0%

commit v1 on v0

--- a/solution.py
+++ b/solution.py
@@ -1,7 +1,193 @@
+import functools
+import itertools
+
 import jax
 import jax.numpy as jnp
 from jax import lax
+from jax.experimental import pallas as pl
+from jax.experimental.pallas import tpu as pltpu
 from jax.sharding import PartitionSpec as P
+MESH = pl.DeviceIdType.MESH
+
+TREES = ("zyx", "zxy", "xyz")
+
+
+def offsets(length):
+    return [0, "o"] if length == 2 else list(range(-(length - 1), length))
+
+
+class Place:
+    def __init__(self, sizes):
+        self.sizes = sizes
+        dp, fs = lax.axis_index("dp"), lax.axis_index("fsdp")
+        self.core = lax.rem(dp, 2)
+        self.pos = {"x": dp // 2, "z": fs // sizes["y"], "y": lax.rem(fs, sizes["y"])}
+
+    def device(self, pos, core):
+        return (pos["x"] * 2 + core, pos["z"] * self.sizes["y"] + pos["y"])
+
+    def index(self, pos, core):
+        dp, fs = self.device(pos, core)
+        return dp * (self.sizes["z"] * self.sizes["y"]) + fs
+
+    def chip(self, pos):
+        return (pos["x"] * self.sizes["z"] + pos["z"]) * self.sizes["y"] + pos["y"]
+
+    def neighbours(self):
+        out = [(None, self.device(self.pos, 1 - self.core))]
+        for d, length in self.sizes.items():
+            if length == 2:
+                out.append((None, self.device({**self.pos, d: 1 - self.pos[d]}, self.core)))
+            elif length > 2:
+                for s in (1, -1):
+                    q = self.pos[d] + s
+                    out.append(((q >= 0) & (q < length), self.device({**self.pos, d: q}, self.core)))
+        return out
+
+
+def when(conds, fn):
+    conds = [c for c in conds if c is not None]
+    if not conds:
+        fn()
+    else:
+        pl.when(functools.reduce(jnp.logical_and, conds))(lambda: (fn(), None)[1])
+
+
+def entry_barrier(place):
+    barrier = pltpu.get_barrier_semaphore()
+    total = 0
+    for cond, dev in place.neighbours():
+        when([cond], lambda dev=dev: pl.semaphore_signal(barrier, inc=1, device_id=dev, device_id_type=MESH))
+        total = total + (1 if cond is None else cond.astype(jnp.int32))
+    pl.semaphore_wait(barrier, total)
+
+
+def gather_kernel(sizes, pieces, order, n_in, *refs):
+    ins, outs = refs[:n_in], refs[n_in:2 * n_in]
+    send_sem, recv_sem, pair_send, pair_recv, local_sem = refs[2 * n_in:]
+    place = Place(sizes)
+    pos, core = place.pos, place.core
+    entry_barrier(place)
+    partner = place.device(pos, 1 - core)
+    locals_ = []
+    for a in range(n_in):
+        c = pltpu.make_async_copy(ins[a], outs[a].at[pos["x"], core, pos["z"], pos["y"]], local_sem.at[a])
+        c.start()
+        locals_.append(c)
+
+    def part(pi, at, who):
+        a, tree, lo, n = pieces[pi]
+        return outs[a].at[at["x"], who, at["z"], at["y"], pl.ds(lo, n)]
+
+    def remote(src, dst, send, recv, dev):
+        return pltpu.make_async_remote_copy(src_ref=src, dst_ref=dst, send_sem=send, recv_sem=recv, device_id=dev, device_id_type=MESH)
+
+    def line(d):
+        if sizes[d] == 1:
+            return []
+        if sizes[d] == 2:
+            return [(0, None, 1 - pos[d])]
+        return [(0, pos[d] + 1 < sizes[d], pos[d] + 1), (1, pos[d] > 0, pos[d] - 1)]
+
+    left = {}
+    for pi, t in order:
+        left[pi] = left.get(pi, 0) + 1
+    seen = dict.fromkeys(left, 0)
+    whole = [slice(None)] * 3
+    for pi, t in order:
+        a, tree, lo, n = pieces[pi]
+        own = all(v == 0 for v in t)
+        at, conds = dict(pos), []
+        for d, v in zip(tree, t):
+            if v == "o":
+                at[d] = 1 - pos[d]
+            elif v != 0:
+                at[d] = pos[d] + v
+                conds.append((at[d] >= 0) if v < 0 else (at[d] < sizes[d]))
+        chip = place.chip(at)
+        dst = part(pi, at, core)
+        src = ins[a].at[pl.ds(lo, n)] if own else dst
+        k = max([j for j, v in enumerate(t) if v != 0], default=-1)
+
+        def handle(tree=tree, t=t, own=own, chip=chip, dst=dst, src=src, k=k, pi=pi):
+            if not own:
+                remote(dst, dst, pair_send.at[pi], recv_sem.at[pi, chip], partner).wait_recv()
+            for j in (2, 1, 0):
+                d = tree[j]
+                if j < k:
+                    continue
+                for slot, ok, q in line(d):
+                    if j == k and (t[j] == "o" or (t[j] < 0) != (slot == 0)):
+                        continue
+                    when([ok], remote(src, dst, send_sem.at[pi, 2 * "xyz".index(d) + slot], recv_sem.at[pi, chip],
+                                      place.device({**pos, d: q}, core)).start)
+            remote(src, dst, pair_send.at[pi], pair_recv.at[pi], partner).start()
+        when(conds, handle)
+        seen[pi] += 1
+
+    full = dict.fromkeys("xyz", slice(None))
+    for pi, (a, tree, lo, n) in enumerate(pieces):
+        for j, d in enumerate(tree):
+            at = {e: (slice(None) if tree.index(e) < j else pos[e]) for e in "xyz"}
+            for slot, ok, q in line(d):
+                sem = send_sem.at[pi, 2 * "xyz".index(d) + slot]
+                if sizes[d] == 2:
+                    ref = part(pi, at, core)
+                    remote(ref, ref, sem, recv_sem.at[pi, 0], partner).wait_send()
+                else:
+                    for z in range(sizes[d]):
+                        ref = part(pi, {**at, d: z}, core)
+                        sent = (pos[d] >= z) if slot == 0 else (pos[d] <= z)
+                        when([ok, sent], remote(ref, ref, sem, recv_sem.at[pi, 0], partner).wait_send)
+        ref = part(pi, full, core)
+        remote(ref, ref, pair_send.at[pi], pair_recv.at[pi], partner).wait_send()
+        ref = part(pi, full, 1 - core)
+        remote(ref, ref, pair_send.at[pi], pair_recv.at[pi], partner).wait_recv()
+    for c in locals_:
+        c.wait()
+
+
+def gather_order(sizes, pieces, alpha):
+    ev = []
+    for pi, (a, tree, lo, n) in enumerate(pieces):
+        for t in itertools.product(*[offsets(sizes[d]) for d in tree]):
+            hops = sum(1 if v == "o" else abs(v) for v in t)
+            ev.append((pi * alpha + hops, pi, t))
+    ev.sort(key=lambda e: (e[0], e[1]))
+    return [(pi, t) for _, pi, t in ev]
+
+
+def gather(sizes, shards, alpha=0.05):
+    chips = sizes["x"] * sizes["y"] * sizes["z"]
+    pieces = []
+    for a, s in enumerate(shards):
+        tiles = s.shape[0] // 8
+        if tiles % 3 == 0 and tiles < 12:
+            cuts = [(i, i * tiles // 3, tiles // 3) for i in range(3)]
+        elif tiles % 2 == 0:
+            cuts = [(i, i * tiles // 2, tiles // 2) for i in range(2)]
+        else:
+            cuts = [(2, 0, tiles)]
+        for tree, lo, n in cuts:
+            pieces.append((a, TREES[tree], lo * 8, n * 8))
+    order = gather_order(sizes, pieces, alpha)
+    n_in = len(shards)
+    return pl.pallas_call(
+        functools.partial(gather_kernel, sizes, pieces, order, n_in),
+        out_shape=[jax.ShapeDtypeStruct((sizes["x"], 2, sizes["z"], sizes["y"]) + s.shape, s.dtype) for s in shards],
+        in_specs=[pl.BlockSpec(memory_space=pltpu.VMEM)] * n_in,
+        out_specs=[pl.BlockSpec(memory_space=pl.ANY)] * n_in,
+        scratch_shapes=[
+            pltpu.SemaphoreType.DMA((len(pieces), 6)),
+            pltpu.SemaphoreType.DMA((len(pieces), chips)),
+            pltpu.SemaphoreType.DMA((len(pieces),)),
+            pltpu.SemaphoreType.DMA((len(pieces),)),
+            pltpu.SemaphoreType.DMA((n_in,)),
+        ],
+        compiler_params=pltpu.CompilerParams(collective_id=0, has_side_effects=True),
+        name="gather",
+    )(*shards)
+
 
 HEAD_DIM = 64
 PASSES = 4
@@ -44,6 +230,27 @@
         lax.all_gather(proj_weight, ("dp", "fsdp"), axis=0, tiled=True),
         lax.all_gather(proj_bias, ("dp", "fsdp"), axis=0, tiled=True),
     )
+
+
+def fetch_all(sizes, attention, mlp):
+    ln1_gain, ln1_bias, qkv_weight, qv_bias, out_weight, out_bias = attention
+    ln2_gain, ln2_bias, fc_weight, fc_bias, proj_weight, proj_bias = mlp
+    big = (qkv_weight, out_weight, fc_weight, proj_weight)
+    small = (ln1_gain, ln1_bias, qv_bias, out_bias, ln2_gain, ln2_bias, fc_bias, proj_bias)
+    width = -(-sum(v.shape[0] for v in small) // 1024) * 128
+    if any(w.shape[0] % 8 for w in big):
+        return fetch_attention(*attention), fetch_mlp(*mlp)
+    packed = jnp.concatenate(small)
+    packed = jnp.pad(packed, (0, 8 * width - packed.shape[0])).reshape(8, width)
+    *full, rows = gather(sizes, (*big, packed))
+    qkv_full, out_full, fc_full, proj_full = [w.reshape(-1, w.shape[-1]) for w in full]
+    rows = rows.reshape(-1, 8 * width)
+    vectors, start = [], 0
+    for v in small:
+        vectors.append(rows[:, start : start + v.shape[0]].reshape(-1))
+        start += v.shape[0]
+    g1, b1, qv, ob, g2, b2, fb, pb = vectors
+    return (g1, b1, qkv_full, qv, out_full, ob), (g2, b2, fc_full, fb, proj_full, pb)
 
 
 def allowed_rows(key_valid, block_rows, seq_len):
@@ -246,6 +453,7 @@
 
 
 def body(
+    sizes,
     hidden,
     sections,
     lengths,
@@ -269,16 +477,15 @@
     key_pos = jnp.arange(seq_len, dtype=jnp.int32)
     key_valid = (key_pos[None, :] < lengths[:, None]) & (token_mask == 1)
 
-    def gather_both():
-        return (
-            fetch_attention(ln1_gain, ln1_bias, qkv_weight, qv_bias, out_weight, out_bias),
-            fetch_mlp(ln2_gain, ln2_bias, fc_weight, fc_bias, proj_weight, proj_bias),
-        )
+    current = fetch_all(
+        sizes,
+        (ln1_gain, ln1_bias, qkv_weight, qv_bias, out_weight, out_bias),
+        (ln2_gain, ln2_bias, fc_weight, fc_bias, proj_weight, proj_bias),
+    )
 
     state = hidden.reshape(row_count, model_width).astype(jnp.float32)
     records = []
     for section_index in range(PASSES):
-        current = gather_both()
         live = jnp.repeat(sections >= section_index, seq_len)[:, None]
         state, record = forward_pass(state, current, key_valid, live, seq_count, seq_len)
         records.append(record)
@@ -287,7 +494,6 @@
     attention_sum = None
     mlp_sum = None
     for section_index in reversed(range(PASSES)):
-        current = gather_both()
         live = jnp.repeat(sections >= section_index, seq_len)[:, None]
         grad_middle, mlp_terms = backward_mlp(grad_state, records[section_index], current, live)
         if mlp_sum is None:
@@ -305,18 +511,18 @@
     attention_grads = (
         lax.psum_scatter(sum_gain_one, ("dp", "fsdp"), scatter_dimension=0, tiled=True),
         lax.psum_scatter(sum_shift_one, ("dp", "fsdp"), scatter_dimension=0, tiled=True),
-        lax.psum_scatter(sum_qkv_w, ("dp", "fsdp"), scatter_dimension=0, tiled=True),
+        lax.psum_scatter(sum_qkv_w.astype(jnp.bfloat16), ("dp", "fsdp"), scatter_dimension=0, tiled=True).astype(jnp.float32),
         lax.psum_scatter(sum_qv_b, ("dp", "fsdp"), scatter_dimension=0, tiled=True),
-        lax.psum_scatter(sum_out_w, ("dp", "fsdp"), scatter_dimension=0, tiled=True),
+        lax.psum_scatter(sum_out_w.astype(jnp.bfloat16), ("dp", "fsdp"), scatter_dimension=0, tiled=True).astype(jnp.float32),
         lax.psum_scatter(sum_out_b, ("dp", "fsdp"), scatter_dimension=0, tiled=True),
     )
     sum_gain_two, sum_shift_two, sum_fc_w, sum_fc_b, sum_proj_w, sum_proj_b = mlp_sum
     finished = (
         lax.psum_scatter(sum_gain_two, ("dp", "fsdp"), scatter_dimension=0, tiled=True),
         lax.psum_scatter(sum_shift_two, ("dp", "fsdp"), scatter_dimension=0, tiled=True),
-        lax.psum_scatter(sum_fc_w, ("dp", "fsdp"), scatter_dimension=0, tiled=True),
+        lax.psum_scatter(sum_fc_w.astype(jnp.bfloat16), ("dp", "fsdp"), scatter_dimension=0, tiled=True).astype(jnp.float32),
         lax.psum_scatter(sum_fc_b, ("dp", "fsdp"), scatter_dimension=0, tiled=True),
-        lax.psum_scatter(sum_proj_w, ("dp", "fsdp"), scatter_dimension=0, tiled=True),
+        lax.psum_scatter(sum_proj_w.astype(jnp.bfloat16), ("dp", "fsdp"), scatter_dimension=0, tiled=True).astype(jnp.float32),
         lax.psum_scatter(sum_proj_b, ("dp", "fsdp"), scatter_dimension=0, tiled=True),
     )
     grad_hidden = grad_state.reshape(seq_count, seq_len, model_width)
@@ -339,8 +545,10 @@
 
 
 def solution(mesh):
+    chips_x = mesh.shape["dp"] // 2
+    sizes = {"x": chips_x, "y": chips_x, "z": mesh.shape["fsdp"] // chips_x}
     return jax.shard_map(
-        body,
+        functools.partial(body, sizes),
         mesh=mesh,
         in_specs=(
             P(("dp", "fsdp"), None, None),

time: 904 us -> 662 us (0.73)
  waiting for transfers between devices: 558 us -> 275 us
  Pallas kernels: 0 us -> 62.8 us
  blocking collectives: 83 us -> 38.5 us
    all_gather x4 -> x0, waiting for transfers between devices: 184 us -> none  [the longest x1 62.8 us: fetch_mlp(): lax.all_gather(fc_weight, ('dp', 'fsdp'), axis=0, tiled=True)]
    reduce_scatter x4, waiting for transfers between devices: 371 us -> 275 us  [the longest x1 110 us: body(): lax.psum_scatter(sum_proj_w.astype(jnp.bfloat16), ('dp', 'fsdp'), scatter...]
    pallas_call x0 -> x1, Pallas kernels: none -> 62.8 us  [gather(): pl.pallas_call(functools.partial(gather_kernel, sizes, pieces, order, n_i...]
    unnamed x2 -> x1, blocking collectives: 83 us -> 38.5 us
    unnamed x528 -> x527, local copies, waits for them, and re-layouts: 22.4 us -> 19.5 us
  transfers between devices with their start and end apart: 8 -> 4, of which waited for: 7 -> 3; matrix products, arithmetic and copies ran while one was open for 12% -> 17% of each run, Pallas kernels for 0% -> 0%
where the time goes in v1:
time: 662 us; the launch traced here: 651 us
  waiting for transfers between devices  275 us (42%)
  matrix products  171 us (26%)
  Pallas kernels  62.8 us (9%)
  local copies, waits for them, and re-layouts  54.3 us (8%)
  blocking collectives  38.5 us (6%)
  other arithmetic  29.9 us (5%)
  between operations  18.6 us (3%)
    reduce_scatter x1, waiting for transfers between devices, body(): lax.psum_scatter(sum_proj_w.astype(jnp.bfloat16), ('dp', 'fsdp'), scatter...  110 us
    reduce_scatter x1, waiting for transfers between devices, body(): lax.psum_scatter(sum_fc_w.astype(jnp.bfloat16), ('dp', 'fsdp'), scatter_d...  110 us
    pallas_call x1, Pallas kernels, gather(): pl.pallas_call(functools.partial(gather_kernel, sizes, pieces, order, n_i...  62.8 us
    reduce_scatter x1, waiting for transfers between devices, body(): lax.psum_scatter(sum_qkv_w.astype(jnp.bfloat16), ('dp', 'fsdp'), scatter_...  54.8 us
    unnamed x1, blocking collectives  38.5 us
    dot_general x4, matrix products, backward_mlp(): jnp.einsum('ti,to->io', activated, grad_branch, preferred_element_type=jn...  29.7 us
    dot_general x4, matrix products, backward_mlp(): jnp.einsum('td,tf->df', normed_two, grad_upper, preferred_element_type=jn...  23.7 us
    unnamed x527, local copies, waits for them, and re-layouts  19.5 us
  transfers between devices with their start and end apart: 4, of which 3 were waited for; matrix products, arithmetic and copies ran while one was open for 17% of the time, Pallas kernels for 0%

profile of v1, /device:TPU:0, one launch (start us, length us, event | category | flops | bytes accessed | tf_op | source)
XLA Modules:
  0.0 650.9 jit_solution(13334288404595134325)
XLA Ops:
  7.2 5.5 concatenate.58
  13.3 62.8 %gather.1 = (bf16[2,2,4,2,24,2304]{5,4,3,2,1,0:T(8,128)(2,1)}, bf16[2,2,4,2,24,768]{5,4,3,2,1,0:T(8,128)(2,1)}, bf16[2,2,4,2,24,3072]{5,4,3,2,1,0:T(8,128)(2,1)}...) custom-call(bf16[24,2304]{1,0:T(8,128)(2,1)} %refs_0_.1, bf16[24,768]{1,0:T(8,128)(2,1)} %refs_1_.1, ...), custom_call_target="tpu_custom_call" | custom-call | tf_op jit(solution)/shard_map/gather/pallas_call | solution.py:175
  83.5 2.7 fusion
  87.8 1.4 copy-done.1
  91.0 4.1 fusion.173
  96.5 1.5 fusion.1
  98.0 2.6 copy.93
  102.8 1.4 convolution_convert_fusion.7
  105.0 3.2 convolution_add_fusion.6
  108.3 4.1 fusion.175
  113.7 1.5 fusion.2
  115.2 2.1 copy.95
  119.5 1.4 convolution_convert_fusion.6
  121.7 3.2 convolution_add_fusion.5
  125.0 4.1 fusion.177
  130.4 1.5 fusion.3
  132.0 2.1 copy.97
  138.5 3.3 convolution_add_fusion.4
  141.9 6.0 convert_reduce_fusion.3
  147.9 2.3 multiply_reduce_fusion.7
  153.9 1.7 copy.99
  155.7 1.6 convolution_bitcast_fusion.2
  157.3 1.4 multiply_reduce_fusion.3
  160.7 2.0 multiply_reduce_fusion.10
  164.1 5.8 convert_reduce_fusion.2
  170.0 2.3 multiply_reduce_fusion.6
  175.2 1.7 copy.103
  176.9 1.6 convolution_bitcast_fusion.1
  178.6 1.4 multiply_reduce_fusion.2
  182.0 2.0 multiply_reduce_fusion.9
  185.6 3.2 convert_reduce_fusion.1
  188.8 2.3 multiply_reduce_fusion.5
  194.0 1.7 copy.107
  195.8 1.6 convolution_bitcast_fusion
  197.4 1.4 multiply_reduce_fusion.1
  203.1 2.0 multiply_reduce_fusion.8
  206.7 3.0 convert_reduce_fusion
  209.8 2.3 multiply_reduce_fusion.4
  213.8 1.5 add_convert_fusion.3
  217.1 2.6 convolution_convert_fusion.1
  219.7 1.7 copy.111
  221.5 1.7 fusion.51
  223.2 1.4 multiply_reduce_fusion
  229.9 4.1 fusion.147
  234.0 6.6 %add_convert_fusion.2 = bf16[768,2304]{1,0:T(8,128)(2,1)} fusion(f32[768,2304]{1,0:T(8,128)S(1)} %fusion.143, f32[768,2304]{1,0:T(8,128)} %fusion.147, f32[768,2304]{1,0:T(8,128)S(1)} %fusion.145, bf16[128,2304]{0,1:T(8,128)(2,1)S(1)} %bitcast.386, bf16[1,128,768]{2,1,0:T(8,128)(2,1)S(1)} %copy-done.32, f32[768]{0:T(1024)S(1)} %copy-done.120, ...), kind=kOutput, calls=%fused_computation.2 | convolution fusion | flops 460652544 | bytes 25566208 | tf_op jit(solution)/shard_map/td,tk->dk/dot_general | solution.py:444
  240.7 6.8 %fusion.149 = f32[3072,768]{1,0:T(8,128)} fusion(bf16[128,768]{1,0:T(8,128)(2,1)} %copy-done.123, f32[128,3072]{1,0:T(8,128)} %copy-done.45), kind=kOutput, calls=%fused_computation.367 | convolution fusion | flops 607518720 | bytes 11206656 | tf_op jit(solution)/shard_map/ti,to->io/dot_general | solution.py:393
  247.5 5.1 fusion.150
  252.7 5.1 fusion.116
  257.8 12.6 %add_convert_fusion = bf16[3072,768]{1,0:T(8,128)(2,1)} fusion(f32[3072,768]{1,0:T(8,128)} %fusion.149, f32[3072,768]{1,0:T(8,128)} %fusion.116, f32[3072,768]{1,0:T(8,128)} %fusion.150, bf16[128,768]{1,0:T(8,128)(2,1)S(1)} %copy-done.125, f32[128,3072]{1,0:T(8,128)S(1)} %copy-done.52), kind=kOutput, calls=%fused_computation | convolution fusion | flops 616955904 | bytes 34799616 | tf_op jit(solution)/shard_map/ti,to->io/dot_general | solution.py:393
  271.1 2.9 fusion.144
  274.0 5.2 fusion.146
  279.3 5.1 fusion.148
  284.4 10.5 %add_convert_fusion.1 = bf16[768,3072]{1,0:T(8,128)(2,1)} fusion(f32[768,3072]{1,0:T(8,128)S(1)} %fusion.144, f32[768,3072]{1,0:T(8,128)} %fusion.148, f32[768,3072]{1,0:T(8,128)} %fusion.146, bf16[128,3072]{1,0:T(8,128)(2,1)} %copy-done.78, f32[128,768]{1,0:T(8,128)} %copy-done.28, f32[768]{0:T(1024)S(1)} %copy-done.115, f32[768]{0:T(1024)S(1)} %copy-done.95, ...), kind=kOutput, calls=%fused_computation.1 | convolution fusion | flops 613908480 | bytes 34216960 | tf_op jit(solution)/shard_map/td,tf->df/dot_general | solution.py:400
  309.4 2.5 fusion.151
  312.9 38.5 %all-reduce.9 = (f32[768]{0:T(1024)S(1)}, f32[768]{0:T(1024)S(1)}, f32[1536]{0:T(1024)S(1)}, f32[768]{0:T(1024)S(1)}, f32[768]{0:T(1024)S(1)}, /*index=5*/f32[76...) all-reduce(f32[768]{0:T(1024)S(1)} %get-tuple-element.162, ...), channel_id=2, replica_groups=mesh['dp'=4,'fsdp'=8] {'dp','fsdp'}, use_global_device_ids=true, to_apply=%region_48.49.clone | all-reduce | flops 9216 | bytes 73728
  356.1 2.3 add_bitcast_fusion
  358.5 4.1 fusion.52
  362.5 1.4 convert_element_type.625
  363.9 54.8 %reduce-scatter.5.cloned.1.call-done = bf16[24,2304]{1,0:T(8,128)(2,1)} async-done(((bf16[768,2304]{1,0:T(8,128)(2,1)}), bf16[24,2304]{1,0:T(8,128)(2,1)}) %reduce-scatter.5.cloned.1.call-update) | async-done | bytes 110608 | tf_op jit(solution)/shard_map/reduce_scatter | solution.py:514
  418.7 1.6 convert_element_type.619
  420.3 110.5 %reduce-scatter.11.cloned.1.call-done = bf16[96,768]{1,0:T(8,128)(2,1)} async-done(((bf16[3072,768]{1,0:T(8,128)(2,1)}), bf16[96,768]{1,0:T(8,128)(2,1)}) %reduce-scatter.11.cloned.1.call-update) | async-done | bytes 147472 | tf_op jit(solution)/shard_map/reduce_scatter | solution.py:525
  530.7 1.6 convert_element_type.638
  532.4 110.2 %reduce-scatter.9.cloned.1.call-done = bf16[24,3072]{1,0:T(8,128)(2,1)} async-done(((bf16[768,3072]{1,0:T(8,128)(2,1)}), bf16[24,3072]{1,0:T(8,128)(2,1)}) %reduce-scatter.9.cloned.1.call-update) | async-done | bytes 147472 | tf_op jit(solution)/shard_map/reduce_scatter | solution.py:523
  642.6 1.6 convert_element_type.631
  (676 shorter events, 74.4 us)
Async XLA Ops:
  7.2 76.3 %copy-start.30 = (bf16[1,128,768]{2,1,0:T(8,128)(2,1)S(1)}, bf16[1,128,768]{2,1,0:T(8,128)(2,1)}, u32[]{:S(2)}) copy-start(bf16[1,128,768]{2,1,0:T(8,128)(2,1)} %param.17) | copy-start | bytes 589828
  7.2 355.3 %reduce-scatter.7.cloned.1.call-start = ((), (), s32[]{:S(2)}) async-start(), calls=%async_computation.5 | async-start | bytes 1216512 | tf_op jit(solution)/shard_map/reduce_scatter | solution.py:516
  81.7 8.3 %slice-start = ((s8[4718592]{0:T(1024)(128)(4,1)}), s8[524288]{0:T(1024)(128)(4,1)S(1)}, s32[]{:S(2)}) async-start(s8[4718592]{0:T(1024)(128)(4,1)} %bitcast.349), calls=%async_computation.8 | async-start | bytes 1048576
  81.7 8.2 %copy-start.134 = (f32[3072]{0:T(1024)}, f32[3072]{0:T(1024)S(1)}, u32[]{:S(2)}) copy-start(f32[3072]{0:T(1024)S(1)} %reshape.1204) | copy-start | bytes 36868
  81.8 8.1 %copy-start.88 = (f32[768]{0:T(1024)}, f32[768]{0:T(1024)S(1)}, u32[]{:S(2)}) copy-start(f32[768]{0:T(1024)S(1)} %reshape.1202) | copy-start | bytes 9220
  81.9 4.3 copy-start.79
  82.0 7.9 %copy-start.111 = (f32[768]{0:T(1024)}, f32[768]{0:T(1024)S(1)}, u32[]{:S(2)}) copy-start(f32[768]{0:T(1024)S(1)} %reshape.1203) | copy-start | bytes 9220
  82.9 4.9 copy-start.146
  90.9 4.2 copy-start.50
  90.9 5.5 copy-start
  90.9 5.5 copy-start.80
  90.9 5.5 copy-start.117
  91.0 5.5 copy-start.139
  108.2 4.1 copy-start.45
  108.3 5.4 copy-start.81
  108.3 5.4 copy-start.118
  108.3 5.4 copy-start.140
  125.0 4.1 copy-start.47
  125.0 5.4 copy-start.82
  125.0 5.4 copy-start.119
  125.0 5.4 copy-start.141
  137.7 4.2 copy-start.132
  138.2 12.1 %copy-start.20 = (f32[128,768]{1,0:T(8,128)}, f32[128,768]{1,0:T(8,128)S(1)}, u32[]{:S(2)}) copy-start(f32[128,768]{1,0:T(8,128)S(1)} %get-tuple-element.140) | copy-start | bytes 1179652
  138.2 12.0 %copy-start.163 = (f32[128]{0:T(128)}, f32[128]{0:T(128)S(1)}, u32[]{:S(2)}) copy-start(f32[128]{0:T(128)S(1)} %broadcast_multiply_fusion) | copy-start | bytes 1540
  138.5 11.8 %copy-start.201 = (f32[128]{0:T(128)}, f32[128]{0:T(128)S(1)}, u32[]{:S(2)}) copy-start(f32[128]{0:T(128)S(1)} %fusion.129) | copy-start | bytes 1540
  138.5 9.4 %slice-start.2 = ((s8[4718592]{0:T(1024)(128)(4,1)}), s8[4194304]{0:T(1024)(128)(4,1)S(1)}, s32[]{:S(2)}) async-start(s8[4718592]{0:T(1024)(128)(4,1)} %bitcast.352), calls=%async_computation.10 | async-start | bytes 8388608
  141.9 6.1 copy-start.42
  141.9 6.0 slice-start.3
  162.7 7.2 %slice-start.4 = ((s8[4718592]{0:T(1024)(128)(4,1)}), s8[4194304]{0:T(1024)(128)(4,1)S(1)}, s32[]{:S(2)}) async-start(s8[4718592]{0:T(1024)(128)(4,1)} %bitcast.355), calls=%async_computation.12 | async-start | bytes 8388608
  163.7 6.1 copy-start.121
  163.8 8.8 %copy-start.62 = (f32[128,768]{1,0:T(8,128)}, f32[128,768]{1,0:T(8,128)S(1)}, u32[]{:S(2)}) copy-start(f32[128,768]{1,0:T(8,128)S(1)} %get-tuple-element.59) | copy-start | bytes 1179652
  164.1 5.8 slice-start.5
  164.1 5.8 copy-start.26
  164.1 5.8 copy-start.92
  164.1 5.8 copy-start.158
  164.1 5.8 copy-start.196
  184.0 4.8 slice-start.6
  185.0 6.4 copy-start.60
  205.1 4.6 slice-start.8
  206.2 6.2 copy-start.70
  215.3 203.4 %reduce-scatter.5.cloned.1.call-start = ((), (), s32[]{:S(2)}) async-start(), calls=%async_computation.4 | async-start | bytes 3649536 | tf_op jit(solution)/shard_map/reduce_scatter | solution.py:514
  229.9 4.1 copy-start.59
  229.9 4.1 copy-start.32
  229.9 4.1 copy-start.153
  229.9 4.1 copy-start.217
  240.6 290.1 %reduce-scatter.11.cloned.1.call-start = ((), (), s32[]{:S(2)}) async-start(), calls=%async_computation.7 | async-start | bytes 4866048 | tf_op jit(solution)/shard_map/reduce_scatter | solution.py:525
  240.6 6.8 %copy-start.49 = (f32[128,3072]{1,0:T(8,128)S(1)}, f32[128,3072]{1,0:T(8,128)}, u32[]{:S(2)}) copy-start(f32[128,3072]{1,0:T(8,128)} %copy-done.47) | copy-start | bytes 4718596
  240.7 6.8 %copy-start.122 = (bf16[128,768]{1,0:T(8,128)(2,1)S(1)}, bf16[128,768]{1,0:T(8,128)(2,1)}, u32[]{:S(2)}) copy-start(bf16[128,768]{1,0:T(8,128)(2,1)} %copy-done.121) | copy-start | bytes 589828
  247.5 5.2 copy-start.43
  247.5 5.2 copy-start.103
  252.7 5.2 copy-start.52
  252.7 5.2 copy-start.125
  270.4 372.2 %reduce-scatter.9.cloned.1.call-start = ((), (), s32[]{:S(2)}) async-start(), calls=%async_computation.6 | async-start | bytes 4866048 | tf_op jit(solution)/shard_map/reduce_scatter | solution.py:523
  274.0 5.3 copy-start.21
  274.0 5.3 copy-start.74
  274.0 5.2 copy-start.164
  274.0 5.2 copy-start.202
  279.3 5.1 copy-start.211
  279.3 5.1 copy-start.221
  294.9 14.2 %copy-start.87 = (f32[768]{0:T(1024)S(1)}, f32[768]{0:T(1024)}, u32[]{:S(2)}) copy-start(f32[768]{0:T(1024)} %copy-done.79) | copy-start | bytes 9220
  311.9 46.5 %copy-start.11 = (f32[128,768]{1,0:T(8,128)S(1)}, f32[128,768]{1,0:T(8,128)}, u32[]{:S(2)}) copy-start(f32[128,768]{1,0:T(8,128)} %copy-done.7) | copy-start | bytes 1179652
  311.9 46.5 %copy-start.22 = (f32[128,768]{1,0:T(8,128)S(1)}, f32[128,768]{1,0:T(8,128)}, u32[]{:S(2)}) copy-start(f32[128,768]{1,0:T(8,128)} %copy-done.20) | copy-start | bytes 1179652
  311.9 46.5 %copy-start.44 = (f32[128,3072]{1,0:T(8,128)S(1)}, f32[128,3072]{1,0:T(8,128)}, u32[]{:S(2)}) copy-start(f32[128,3072]{1,0:T(8,128)} %copy-done.42) | copy-start | bytes 4718596
  311.9 46.5 %copy-start.225 = (f32[768]{0:T(1024)S(1)}, f32[768]{0:T(1024)}, u32[]{:S(2)}) copy-start(f32[768]{0:T(1024)} %reshape.1205) | copy-start | bytes 9220
  (199 other events, 412.4 us)
Sparse Core Ops, SparseCore 0:
  215.4 95.3 reduce-scatter.6
  316.2 102.4 reduce-scatter.4
  424.2 106.5 reduce-scatter.10
  536.1 106.4 reduce-scatter.8
